TPU v7x, 512 devices: a whole 4x4x16 slice. The times are simulated.
512 devices in a mesh: grp: 32 (over y, x, core), shard: 16 (over z).
Axes of the slice: x: 4, y: 4, z: 16, core: 2. Of those that a mesh axis runs over, the one named last changes fastest.
Arguments:
- grads: bfloat16 [2, 32, 16, 768, 768], P(None, 'grp', 'shard')
- vec_grads: bfloat16 [2, 32, 16, 8, 768], P(None, 'grp', 'shard'), may hold values from -0.5 to 0.5
- weight: float32 [768, 768], P('shard'), may hold values from -0.21875 to 0.21875
- basis: float32 [768, 256], replicated, may hold values from -0.21875 to 0.21875
- moment: float32 [768, 256], P('shard'), may hold values from -4 to 4
- second: float32 [768, 256], P('shard'), may hold values from 0.01 to 1
- vectors: float32 [8, 768], P(None, 'shard'), may hold values from -6 to 6
- vec_moment: float32 [8, 768], P(None, 'shard'), may hold values from -1.5 to 1.5
- vec_second: float32 [8, 768], P(None, 'shard'), may hold values from 0.001 to 0.1
Outputs:
- new_weight: float32 [768, 768], P('shard')
- update: bfloat16 [768, 768], P('shard')
- new_moment: float32 [768, 256], P('shard')
- new_second: float32 [768, 256], P('shard')
- new_basis: float32 [768, 256], replicated
- new_vectors: float32 [8, 768], P(None, 'shard')
- new_vec_moment: float32 [8, 768], P(None, 'shard')
- new_vec_second: float32 [8, 768], P(None, 'shard')
All inputs are finite; a program needn't handle non-finite values.
Results may differ from a plain program's by a relative error of at most 0.001.
Values sent between devices are 32-bit elements; how exact they have to be, the bound alone decides.
A program may use at most 64 MiB of HBM per device.

v0:
```python
import jax
import jax.numpy as jnp
from jax import lax
from jax.sharding import PartitionSpec as P

NS_STEPS = 5
STEP = 100
HIGH = lax.Precision.HIGHEST


def matmul(left, right):
    return jnp.dot(left, right, precision=HIGH, preferred_element_type=jnp.float32)


def per_device(grads, vec_grads, weight, basis, moment, second, vectors, vec_moment, vec_second):
    shards = lax.axis_size("shard")
    width = grads.shape[-1]
    rows = weight.shape[0]
    cols = vectors.shape[1]
    me = lax.axis_index("shard")
    summed = grads[0, 0, 0].astype(jnp.float32) + grads[1, 0, 0].astype(jnp.float32)
    vec_local = vec_grads[0, 0, 0].astype(jnp.float32) + vec_grads[1, 0, 0].astype(jnp.float32)
    packed = jnp.concatenate([summed, vec_local], axis=0)
    packed = lax.psum(packed, ("grp", "shard"))
    total = packed[:width]
    vec_total = packed[width:]
    projected_all = matmul(total, basis)
    subspace = lax.dot_general(
        total,
        projected_all,
        (((0,), (0,)), ((), ())),
        precision=HIGH,
        preferred_element_type=jnp.float32,
    )
    squares = jnp.sum(total * total) + jnp.sum(vec_total * vec_total)
    iterate = subspace / jnp.sqrt(jnp.sum(subspace * subspace) + 1e-06)
    for step in range(NS_STEPS):
        gram = matmul(iterate.T, iterate)
        iterate = 1.5 * iterate - 0.5 * matmul(iterate, gram)
    factor = 1.0 / jnp.maximum(jnp.sqrt(squares / (width * width + vec_total.size)), 1.0)
    projected = lax.dynamic_slice_in_dim(projected_all, me * rows, rows, axis=0)
    vec_sum = lax.dynamic_slice_in_dim(vec_total, me * cols, cols, axis=1)
    first_fix = 1.0 - 0.9**STEP
    second_fix = 1.0 - 0.999**STEP
    grad_low = factor * projected
    new_moment = 0.9 * moment + 0.1 * grad_low
    new_second = 0.999 * second + 0.001 * grad_low * grad_low
    normalized = new_moment / first_fix / (jnp.sqrt(new_second / second_fix) + 1e-08)
    full = lax.dot_general(
        normalized,
        basis,
        (((1,), (1,)), ((), ())),
        precision=HIGH,
        preferred_element_type=jnp.float32,
    )
    new_weight = weight - 0.001 * (0.25 * full + 0.01 * weight)
    vec_grad = factor * vec_sum
    new_vec_moment = 0.9 * vec_moment + 0.1 * vec_grad
    new_vec_second = 0.999 * vec_second + 0.001 * vec_grad * vec_grad
    vec_step = new_vec_moment / first_fix / (jnp.sqrt(new_vec_second / second_fix) + 1e-08)
    new_vectors = vectors - 0.001 * (vec_step + 0.01 * vectors)
    return (
        new_weight,
        full.astype(jnp.bfloat16),
        new_moment,
        new_second,
        iterate,
        new_vectors,
        new_vec_moment,
        new_vec_second,
    )


def solution(mesh):
    return jax.shard_map(
        per_device,
        mesh=mesh,
        in_specs=(
            P(None, "grp", "shard", None, None),
            P(None, "grp", "shard", None, None),
            P("shard", None),
            P(),
            P("shard", None),
            P("shard", None),
            P(None, "shard"),
            P(None, "shard"),
            P(None, "shard"),
        ),
        out_specs=(
            P("shard", None),
            P("shard", None),
            P("shard", None),
            P("shard", None),
            P(),
            P(None, "shard"),
            P(None, "shard"),
            P(None, "shard"),
        ),
        check_vma=False,
    )
```

profile of v0, /device:TPU:1, one launch (start us, length us, event | category | flops | bytes accessed | tf_op | source)
XLA Modules:
  0.0 534.5 jit_solution(420021904912794236)
XLA Ops:
  7.2 0.0 copy-start
  7.2 0.0 all-reduce.2.cloned.1.call-start
  7.2 0.8 add_bitcast_fusion.1
  8.0 1.9 add_bitcast_fusion
  9.9 1.6 pad_maximum_fusion
  11.5 0.0 all-reduce.2.cloned.1.call-update
  11.5 485.5 %all-reduce.2.cloned.1.call-done = f32[776,768]{1,0:T(8,128)} async-done(((f32[776,768]{1,0:T(8,128)}), f32[776,768]{1,0:T(8,128)}) %all-reduce.2.cloned.1.call-update) | async-done | bytes 2383888 | tf_op jit(solution)/shard_map/psum | solution.py:24
  497.0 3.0 multiply_reduce_fusion
  500.0 1.3 fusion.25
  502.7 2.0 fusion.2
  504.8 5.3 multiply_reduce_fusion.1
  510.9 2.9 fusion.9
  513.8 0.8 fusion.8
  514.6 1.4 fusion.27
  516.0 0.8 fusion.7
  516.8 1.6 fusion.28
  518.4 0.8 fusion.6
  519.2 1.4 fusion.29
  520.7 0.8 fusion.5
  521.5 1.4 fusion.30
  522.9 1.7 fusion.4
  524.6 0.8 multiply_add_fusion
  525.5 1.5 fusion.26
  527.0 0.7 multiply_subtract_fusion.1
  (23 shorter events, 0.1 us)
Async XLA Ops:
  7.2 495.5 %copy-start = (f32[768,256]{1,0:T(8,128)S(1)}, f32[768,256]{1,0:T(8,128)}, u32[]{:S(2)}) copy-start(f32[768,256]{1,0:T(8,128)} %param.12) | copy-start | bytes 2359300
  7.2 489.8 %all-reduce.2.cloned.1.call-start = ((), (), s32[]{:S(2)}) async-start(), calls=%async_computation | async-start | bytes 4767744 | tf_op jit(solution)/shard_map/psum | solution.py:24
  497.0 5.8 %copy-start.1 = (f32[776,768]{1,0:T(8,128)S(1)}, f32[776,768]{1,0:T(8,128)}, u32[]{:S(2)}) copy-start(f32[776,768]{1,0:T(8,128)} %all-reduce.2.cloned.1.call-done) | copy-start | bytes 7151620
  504.7 5.3 %copy-start.2 = (f32[768,256]{1,0:T(8,128)}, f32[768,256]{1,0:T(8,128)S(1)}, u32[]{:S(2)}) copy-start(f32[768,256]{1,0:T(8,128)S(1)} %fusion.2) | copy-start | bytes 2359300
  510.1 3.7 copy-start.3
  520.6 4.0 copy-start.7
  520.6 4.0 copy-start.8
  521.4 4.0 copy-start.6
  521.5 5.5 %copy-start.9 = (f32[8,48]{1,0:T(8,128)S(1)}, f32[8,48]{1,0:T(8,128)}, u32[]{:S(2)}) copy-start(f32[8,48]{1,0:T(8,128)} %param.15) | copy-start | bytes 4612
  521.5 5.5 %copy-start.10 = (f32[8,48]{1,0:T(8,128)S(1)}, f32[8,48]{1,0:T(8,128)}, u32[]{:S(2)}) copy-start(f32[8,48]{1,0:T(8,128)} %param.16) | copy-start | bytes 4612
  521.5 5.5 %copy-start.11 = (f32[8,48]{1,0:T(8,128)S(1)}, f32[8,48]{1,0:T(8,128)}, u32[]{:S(2)}) copy-start(f32[8,48]{1,0:T(8,128)} %param.17) | copy-start | bytes 4612
  525.4 2.3 copy-start.4
  525.4 2.3 copy-start.5
Sparse Core Ops, SparseCore 0:
  13.4 483.5 all-reduce.1
where the time goes:
time: 535 us
  waiting for transfers between devices  485 us (91%)
  matrix products  22.4 us (4%)
  between operations  16.4 us (3%)
  other arithmetic  10.1 us (2%)
    psum x1, waiting for transfers between devices, per_device(): packed = lax.psum(packed, ('grp', 'shard'))  485 us
    dot_general x11, matrix products, matmul(): jnp.dot(left, right, precision=HIGH, preferred_element_type=jnp.float32)  15.6 us
  transfers between devices with their start and end apart: 1, of which 1 were waited for; matrix products, arithmetic and copies ran while one was open for 0% of the time, Pallas kernels for 0%

commit v1 on v0

--- a/solution.py
+++ b/solution.py
@@ -21,7 +21,8 @@
     summed = grads[0, 0, 0].astype(jnp.float32) + grads[1, 0, 0].astype(jnp.float32)
     vec_local = vec_grads[0, 0, 0].astype(jnp.float32) + vec_grads[1, 0, 0].astype(jnp.float32)
     packed = jnp.concatenate([summed, vec_local], axis=0)
-    packed = lax.psum(packed, ("grp", "shard"))
+    for name in ("grp", "shard"):
+        packed = lax.psum(packed, name)
     total = packed[:width]
     vec_total = packed[width:]
     projected_all = matmul(total, basis)

time: 535 us -> 342 us (0.64)
  the two profiles are of different devices: /device:TPU:1 before, /device:TPU:2 now
where the time goes in v1:
time: 342 us; the launch traced here: 341 us
  waiting for transfers between devices  292 us (85%)
  matrix products  22.4 us (7%)
  between operations  16.4 us (5%)
  other arithmetic  10.1 us (3%)
    psum x2, waiting for transfers between devices, per_device(): packed = lax.psum(packed, name)  292 us
    dot_general x11, matrix products, matmul(): jnp.dot(left, right, precision=HIGH, preferred_element_type=jnp.float32)  15.6 us
  transfers between devices with their start and end apart: 2, of which 2 were waited for; matrix products, arithmetic and copies ran while one was open for 0% of the time, Pallas kernels for 0%

profile of v1, /device:TPU:2, one launch (start us, length us, event | category | flops | bytes accessed | tf_op | source)
XLA Modules:
  0.0 341.3 jit_solution(7855629543243052)
XLA Ops:
  7.2 0.0 all-reduce.3.cloned.1.call-start
  7.2 0.8 add_bitcast_fusion.1
  8.0 1.9 add_bitcast_fusion
  9.9 1.6 pad_maximum_fusion
  11.5 0.0 all-reduce.5.cloned.1.call-start
  11.5 142.9 %all-reduce.3.cloned.1.call-done = f32[776,768]{1,0:T(8,128)} async-done(((f32[776,768]{1,0:T(8,128)}), f32[776,768]{1,0:T(8,128)}) %all-reduce.3.cloned.1.call-update) | async-done | bytes 2383888 | tf_op jit(solution)/shard_map/psum | solution.py:25
  154.5 149.2 %all-reduce.5.cloned.1.call-done = f32[776,768]{1,0:T(8,128)} async-done(((f32[776,768]{1,0:T(8,128)}), f32[776,768]{1,0:T(8,128)}) %all-reduce.5.cloned.1.call-update) | async-done | bytes 2383888 | tf_op jit(solution)/shard_map/psum | solution.py:25
  303.7 3.0 multiply_reduce_fusion
  306.7 1.3 fusion.25
  309.5 2.0 fusion.2
  311.5 5.3 %multiply_reduce_fusion.1 = (f32[]{:T(128)}, f32[768,256]{1,0:T(8,128)}) fusion(f32[768,256]{1,0:T(8,128)S(1)} %fusion.2, f32[776,768]{1,0:T(8,128)S(1)} %copy-done.1), kind=kOutput, calls=%fused_computation.17 | convolution fusion | flops 1812332544 | bytes 3932164 | tf_op jit(solution)/shard_map/dot_general | solution.py:29
  317.6 2.9 fusion.9
  320.5 0.8 fusion.8
  321.3 1.4 fusion.27
  322.7 0.8 fusion.7
  323.5 1.6 fusion.28
  325.1 0.8 fusion.6
  325.9 1.4 fusion.29
  327.4 0.8 fusion.5
  328.2 1.4 fusion.30
  329.7 1.7 fusion.4
  331.3 0.8 multiply_add_fusion
  332.2 1.5 fusion.26
  333.7 0.7 multiply_subtract_fusion.1
  (26 shorter events, 0.1 us)
Async XLA Ops:
  7.2 302.3 %copy-start = (f32[768,256]{1,0:T(8,128)S(1)}, f32[768,256]{1,0:T(8,128)}, u32[]{:S(2)}) copy-start(f32[768,256]{1,0:T(8,128)} %param.12) | copy-start | bytes 2359300
  7.2 147.2 %all-reduce.3.cloned.1.call-start = ((), (), s32[]{:S(2)}) async-start(), calls=%async_computation | async-start | bytes 4767744 | tf_op jit(solution)/shard_map/psum | solution.py:25
  11.5 292.2 %all-reduce.5.cloned.1.call-start = ((), (), s32[]{:S(2)}) async-start(), calls=%async_computation.1 | async-start | bytes 4767744 | tf_op jit(solution)/shard_map/psum | solution.py:25
  303.7 5.8 %copy-start.1 = (f32[776,768]{1,0:T(8,128)S(1)}, f32[776,768]{1,0:T(8,128)}, u32[]{:S(2)}) copy-start(f32[776,768]{1,0:T(8,128)} %all-reduce.5.cloned.1.call-done) | copy-start | bytes 7151620
  311.5 5.3 %copy-start.2 = (f32[768,256]{1,0:T(8,128)}, f32[768,256]{1,0:T(8,128)S(1)}, u32[]{:S(2)}) copy-start(f32[768,256]{1,0:T(8,128)S(1)} %fusion.2) | copy-start | bytes 2359300
  316.8 3.7 %copy-start.3 = (f32[768,256]{1,0:T(8,128)S(1)}, f32[768,256]{1,0:T(8,128)}, u32[]{:S(2)}) copy-start(f32[768,256]{1,0:T(8,128)} %get-tuple-element.18) | copy-start | bytes 2359300
  327.4 4.0 %copy-start.7 = (f32[48,256]{1,0:T(8,128)S(1)}, f32[48,256]{1,0:T(8,128)}, u32[]{:S(2)}) copy-start(f32[48,256]{1,0:T(8,128)} %param.13) | copy-start | bytes 147460
  327.4 4.0 %copy-start.8 = (f32[48,256]{1,0:T(8,128)S(1)}, f32[48,256]{1,0:T(8,128)}, u32[]{:S(2)}) copy-start(f32[48,256]{1,0:T(8,128)} %param.14) | copy-start | bytes 147460
  328.2 4.0 %copy-start.6 = (f32[48,768]{1,0:T(8,128)S(1)}, f32[48,768]{1,0:T(8,128)}, u32[]{:S(2)}) copy-start(f32[48,768]{1,0:T(8,128)} %param.11) | copy-start | bytes 442372
  328.2 5.5 %copy-start.9 = (f32[8,48]{1,0:T(8,128)S(1)}, f32[8,48]{1,0:T(8,128)}, u32[]{:S(2)}) copy-start(f32[8,48]{1,0:T(8,128)} %param.15) | copy-start | bytes 4612
  328.2 5.5 %copy-start.10 = (f32[8,48]{1,0:T(8,128)S(1)}, f32[8,48]{1,0:T(8,128)}, u32[]{:S(2)}) copy-start(f32[8,48]{1,0:T(8,128)} %param.16) | copy-start | bytes 4612
  328.2 5.5 %copy-start.11 = (f32[8,48]{1,0:T(8,128)S(1)}, f32[8,48]{1,0:T(8,128)}, u32[]{:S(2)}) copy-start(f32[8,48]{1,0:T(8,128)} %param.17) | copy-start | bytes 4612
  332.2 2.3 copy-start.4
  332.2 2.3 copy-start.5
Sparse Core Ops, SparseCore 0:
  11.6 142.7 all-reduce.2
  156.8 146.8 all-reduce.4
